TPU v7x, 512 devices: a whole 4x8x8 slice. The times are simulated.
512 devices in a mesh: seq: 16 (over y, core), doc: 32 (over z, x).
Axes of the slice: x: 4, y: 8, z: 8, core: 2. Of those that a mesh axis runs over, the one named last changes fastest.
Arguments:
- queries: bfloat16 [262144, 512], P(('doc', 'seq')), parts along dimension 0, may hold values from -64 to 64
- keys: bfloat16 [262144, 512], P(('doc', 'seq')), parts along dimension 0, may hold values from -6 to 6
- values: bfloat16 [262144, 512], P(('doc', 'seq')), parts along dimension 0, may hold values from -6 to 6
- rates: float32 [262144], P(('doc', 'seq')), parts along dimension 0, may hold values from 0.1 to 1
- lengths: int32 [128], P('doc'), parts along dimension 0, may hold values from 1 to 4096, 8192 in all
- norm_gain: float32 [16384], P('doc'), parts along dimension 0, may hold values from 0.5 to 1.5
- w_gate: bfloat16 [16384, 512], P('doc'), parts along dimension 0, may hold values from -0.25 to 0.25
- w_up: bfloat16 [16384, 512], P('doc'), parts along dimension 0, may hold values from -0.25 to 0.25
- w_down: bfloat16 [16384, 512], P('doc'), parts along dimension 0, may hold values from -0.25 to 0.25
- mom_gate: float32 [16384, 512], P('doc', 'seq'), parts along dimension 0, may hold values from -3 to 3
- mom_up: float32 [16384, 512], P('doc', 'seq'), parts along dimension 0, may hold values from -3 to 3
- mom_down: float32 [16384, 512], P('doc', 'seq'), parts along dimension 0, may hold values from -3 to 3
Outputs:
- mixed: bfloat16 [262144, 512], P(('doc', 'seq')), parts along dimension 0
- new_mom_gate: float32 [16384, 512], P('doc', 'seq'), parts along dimension 0
- new_mom_up: float32 [16384, 512], P('doc', 'seq'), parts along dimension 0
- new_mom_down: float32 [16384, 512], P('doc', 'seq'), parts along dimension 0
There are 32 independent parts, one for each index of `doc`. A program takes and returns all parts, laid end to end along the dimension named above; each array names one. Nothing has to cross between parts.
All inputs are finite; a program needn't handle non-finite values.
Results may differ from a plain program's by a relative error of at most 0.019.
Values may be sent and summed in bfloat16 or wider, within the bound.
No kernel may reach another device: no remote copies, remote signals or barrier semaphores. Data moves between devices by JAX's collectives and lax.ppermute only.
A program may use at most 64 MiB of HBM per device.

v0:
```python
import jax
import jax.numpy as jnp
from jax import lax
from jax.sharding import PartitionSpec as P

WIN = 1024
momentum_decay = 0.9
step_size = 0.5


def shifted(block, axis, distance):
    devices = range(lax.axis_size(axis))
    route = [(i - distance, i) for i in devices if i - distance in devices]
    return lax.ppermute(block, axis, route)


def doc_ids(positions, ends):
    return jnp.sum((positions[:, None] >= ends[None, :]).astype(jnp.int32), axis=1)


def window_attention(qblk, kblk, vblk, qpos, kpos, ends):
    scores = jnp.dot(qblk, kblk.T, preferred_element_type=jnp.float32) * qblk.shape[1] ** (-0.5)
    same = doc_ids(qpos, ends)[:, None] == doc_ids(kpos, ends)[None, :]
    delta = qpos[:, None] - kpos[None, :]
    live = same & (delta >= 0) & (delta < WIN) & (kpos[None, :] >= 0)
    scores = jnp.where(live, scores, jnp.float32(-1e30))
    top = jnp.max(scores, axis=1, keepdims=True)
    weights = jnp.where(live, jnp.exp(scores - top), jnp.float32(0.0))
    total = jnp.sum(weights, axis=1, keepdims=True)
    probs = (weights / total).astype(jnp.bfloat16)
    return jnp.dot(probs, vblk, preferred_element_type=jnp.float32)


def silu_parts(gate):
    sig = jax.nn.sigmoid(gate)
    return (gate * sig, sig * (1.0 + gate * (1.0 - sig)))


def step_weight(weight, moment):
    normed = moment * lax.rsqrt(jnp.sum(moment * moment, axis=0, keepdims=True) + 1e-06)
    return (weight.astype(jnp.float32) - step_size * normed).astype(jnp.bfloat16)


def local(
    queries,
    keys,
    values,
    rates,
    lengths,
    norm_gain,
    w_gate,
    w_up,
    w_down,
    mom_gate,
    mom_up,
    mom_down,
):
    tok, width = queries.shape
    index = lax.axis_index("seq")
    ends = jnp.cumsum(lengths)
    reach = (WIN + tok - 1) // tok
    paired = jnp.stack((keys, values))
    earlier = [shifted(paired, "seq", hops) for hops in range(reach, 0, -1)]
    buffer = jnp.concatenate(earlier + [paired], axis=1)
    halo_len = reach * tok
    first = index * tok
    begin = halo_len - WIN
    qpos = first + 0 + jnp.arange(tok, dtype=jnp.int32)
    kpos = first + 0 - WIN + jnp.arange(tok + WIN, dtype=jnp.int32)
    pieces = window_attention(
        queries,
        buffer[0, begin : begin + tok + WIN],
        buffer[1, begin : begin + tok + WIN],
        qpos,
        kpos,
        ends,
    )
    gate = jnp.dot(keys, w_gate, preferred_element_type=jnp.float32)
    upper = jnp.dot(keys, w_up, preferred_element_type=jnp.float32)
    act, slope = silu_parts(gate)
    hidden = (act * upper).astype(jnp.bfloat16)
    err = (-(rates[:, None] * values.astype(jnp.float32))).astype(jnp.bfloat16)
    back = jnp.dot(err, w_down.T, preferred_element_type=jnp.float32)
    d_up = (back * act).astype(jnp.bfloat16)
    d_gate = (back * upper * slope).astype(jnp.bfloat16)
    part_gate = jnp.dot(keys.T, d_gate, preferred_element_type=jnp.float32)
    part_up = jnp.dot(keys.T, d_up, preferred_element_type=jnp.float32)
    part_down = jnp.dot(hidden.T, err, preferred_element_type=jnp.float32)
    scale = float(tok * lax.axis_size("seq")) ** (-0.5)
    hid_cols = mom_gate.shape[1]
    out_cols = mom_down.shape[1]
    sum_gate, sum_up, sum_down = (
        lax.psum_scatter(
            part_gate.astype(jnp.bfloat16), "seq", scatter_dimension=1, tiled=True
        ).astype(jnp.float32),
        lax.psum_scatter(
            part_up.astype(jnp.bfloat16), "seq", scatter_dimension=1, tiled=True
        ).astype(jnp.float32),
        lax.psum_scatter(
            part_down.astype(jnp.bfloat16), "seq", scatter_dimension=1, tiled=True
        ).astype(jnp.float32),
    )
    new_mom_gate = momentum_decay * mom_gate + sum_gate * scale
    new_mom_up = momentum_decay * mom_up + sum_up * scale
    new_mom_down = momentum_decay * mom_down + sum_down * scale
    shard_gate = step_weight(
        lax.dynamic_slice_in_dim(w_gate, index * hid_cols, hid_cols, 1), new_mom_gate
    )
    shard_up = step_weight(
        lax.dynamic_slice_in_dim(w_up, index * hid_cols, hid_cols, 1), new_mom_up
    )
    shard_down = step_weight(
        lax.dynamic_slice_in_dim(w_down, index * out_cols, out_cols, 1), new_mom_down
    )
    gate_new, up_new, down_new = (
        lax.all_gather(shard_gate, "seq", axis=1, tiled=True),
        lax.all_gather(shard_up, "seq", axis=1, tiled=True),
        lax.all_gather(shard_down, "seq", axis=1, tiled=True),
    )
    qa = jnp.dot(queries, gate_new, preferred_element_type=jnp.float32)
    qb = jnp.dot(queries, up_new, preferred_element_type=jnp.float32)
    qh = (jax.nn.silu(qa) * qb).astype(jnp.bfloat16)
    fast = jnp.dot(qh, down_new, preferred_element_type=jnp.float32)
    normed = fast * lax.rsqrt(jnp.mean(fast * fast, axis=1, keepdims=True) + 1e-06) * norm_gain
    mixed = (pieces + normed).astype(jnp.bfloat16)
    return (mixed, new_mom_gate, new_mom_up, new_mom_down)


def solution(mesh):
    in_specs = (
        P(("doc", "seq"), None),
        P(("doc", "seq"), None),
        P(("doc", "seq"), None),
        P(("doc", "seq")),
        P("doc"),
        P("doc"),
        P("doc", None),
        P("doc", None),
        P("doc", None),
        P("doc", "seq"),
        P("doc", "seq"),
        P("doc", "seq"),
    )
    out_specs = (P(("doc", "seq"), None), P("doc", "seq"), P("doc", "seq"), P("doc", "seq"))
    return jax.shard_map(local, mesh=mesh, in_specs=in_specs, out_specs=out_specs, check_vma=False)
```

profile of v0, /device:TPU:1, one launch (start us, length us, event | category | flops | bytes accessed | tf_op | source)
XLA Modules:
  0.0 261.2 jit_solution(15479746361720381000)
XLA Ops:
  7.2 0.0 copy-start
  7.2 0.0 reduce-scatter.6.cloned.1.call-start
  7.2 1.7 fusion.32
  9.0 2.1 fusion.23
  11.1 0.0 copy-start.6
  11.1 1.3 fusion.13
  12.4 0.0 reduce-scatter.6.cloned.1.call-update
  12.4 0.0 reduce-scatter.4.cloned.1.call-start
  12.5 0.4 fusion.31
  13.0 1.0 copy-done.5
  13.9 2.9 %fusion.12 = bf16[512,512]{0,1:T(8,128)(2,1)} fusion(bf16[512,512]{1,0:T(8,128)(2,1)S(1)} %copy-done.1, f32[512,512]{1,0:T(8,128)} %copy-done.3, f32[512,512]{1,0:T(8,128)S(1)} %fusion.23, f32[512,512]{1,0:T(8,128)S(1)} %fusion.31), kind=kOutput, calls=%fused_computation.25 | convolution fusion | flops 271319040 | bytes 4194304 | tf_op jit(solution)/shard_map/dot_general | solution.py:86
  16.8 0.0 reduce-scatter.4.cloned.1.call-update
  16.8 0.0 reduce-scatter.8.cloned.1.call-start
  16.9 0.1 pad_maximum_fusion
  17.0 0.0 copy-start.16
  17.0 4.6 %collective-permute-start.1 = (bf16[2,512,512]{2,1,0:T(8,128)(2,1)S(1)}, bf16[2,512,512]{2,1,0:T(8,128)(2,1)}, u32[]{:S(2)}, u32[]{:S(2)}) collective-permute-start(bf16[2,512,512]{2,1,0:T(8,128)(2,1)S(1)} %pad_maximum_fusion), channel_id=1, source_target_pairs={{0,32},{32,64},{64,96},{96,128},{128,160},{160,192},{192,224},{224... | collective-permute-start | bytes 3145736 | tf_op jit(solution)/shard_map/ppermute | solution.py:14
  21.6 4.2 %collective-permute-start = (bf16[2,512,512]{2,1,0:T(8,128)(2,1)S(1)}, bf16[2,512,512]{2,1,0:T(8,128)(2,1)}, u32[]{:S(2)}, u32[]{:S(2)}) collective-permute-start(bf16[2,512,512]{2,1,0:T(8,128)(2,1)S(1)} %pad_maximum_fusion), channel_id=1, source_target_pairs={{0,64},{32,96},{64,128},{96,160},{128,192},{160,224},{192,256},{22... | collective-permute-start | bytes 3145736 | tf_op jit(solution)/shard_map/ppermute | solution.py:14
  25.8 3.1 %convolution_convert_fusion = bf16[512,512]{0,1:T(8,128)(2,1)} fusion(f32[512,512]{1,0:T(8,128)} %copy-done.5, f32[512,512]{1,0:T(8,128)} %copy-done.3, bf16[512,512]{1,0:T(8,128)(2,1)S(1)} %copy-done.2, f32[512]{0:T(512)S(1)} %copy-done.14), kind=kOutput, calls=%fused_computation.20 | convolution fusion | flops 271319040 | bytes 3147776 | tf_op jit(solution)/shard_map/dot_general | solution.py:88
  28.9 0.0 reduce-scatter.8.cloned.1.call-update
  28.9 0.6 broadcast_compare_fusion
  29.5 1.0 constant_dynamic-slice_fusion.2
  30.5 1.0 constant_dynamic-slice_fusion
  31.6 0.2 reduce-window.8
  31.7 0.7 convert_reduce_fusion.1
  32.4 0.1 convert_reduce_fusion
  32.5 0.7 copy.27
  33.2 0.1 copy.29
  33.3 0.1 copy.28
  33.4 42.8 %reduce-scatter.6.cloned.1.call-done = bf16[512,32]{0,1:T(8,128)(2,1)} async-done(((bf16[512,512]{0,1:T(8,128)(2,1)}), bf16[512,32]{0,1:T(8,128)(2,1)}) %reduce-scatter.6.cloned.1.call-update) | async-done | bytes 32784 | tf_op jit(solution)/shard_map/reduce_scatter | solution.py:96
  76.2 1.0 multiply_reduce_fusion.2
  77.2 60.9 %reduce-scatter.4.cloned.1.call-done = bf16[512,32]{0,1:T(8,128)(2,1)} async-done(((bf16[512,512]{0,1:T(8,128)(2,1)}), bf16[512,32]{0,1:T(8,128)(2,1)}) %reduce-scatter.4.cloned.1.call-update) | async-done | bytes 32784 | tf_op jit(solution)/shard_map/reduce_scatter | solution.py:93
  138.1 1.0 multiply_reduce_fusion.3
  139.1 0.1 subtract_convert_fusion.1
  139.2 17.9 %all_gather.10 = bf16[512,512]{0,1:T(8,128)(2,1)S(1)} all-gather(bf16[512,32]{0,1:T(8,128)(2,1)S(1)} %subtract_convert_fusion.1), channel_id=1, replica_groups=mesh['seq'=16,'doc'=32] {'seq'}, dimensions={1}, use_global_device_ids=true | all-gather | bytes 557056 | tf_op jit(solution)/shard_map/all_gather | solution.py:117
  157.1 43.1 %reduce-scatter.8.cloned.1.call-done = bf16[512,32]{0,1:T(8,128)(2,1)} async-done(((bf16[512,512]{0,1:T(8,128)(2,1)}), bf16[512,32]{0,1:T(8,128)(2,1)}) %reduce-scatter.8.cloned.1.call-update) | async-done | bytes 32784 | tf_op jit(solution)/shard_map/reduce_scatter | solution.py:99
  200.2 1.0 multiply_reduce_fusion.1
  201.2 0.1 subtract_convert_fusion
  201.2 19.3 %all_gather.11 = bf16[512,512]{0,1:T(8,128)(2,1)} all-gather(bf16[512,32]{0,1:T(8,128)(2,1)S(1)} %subtract_convert_fusion), channel_id=1, replica_groups=mesh['seq'=16,'doc'=32] {'seq'}, dimensions={1}, use_global_device_ids=true | all-gather | bytes 557056 | tf_op jit(solution)/shard_map/all_gather | solution.py:118
  220.5 0.8 subtract_convert_fusion.2
  221.3 17.4 %all_gather.9 = bf16[512,512]{0,1:T(8,128)(2,1)S(1)} all-gather(bf16[512,32]{0,1:T(8,128)(2,1)S(1)} %subtract_convert_fusion.2), channel_id=1, replica_groups=mesh['seq'=16,'doc'=32] {'seq'}, dimensions={1}, use_global_device_ids=true | all-gather | bytes 557056 | tf_op jit(solution)/shard_map/all_gather | solution.py:116
  238.7 1.5 convolution_bitcast_fusion.1
  240.2 3.3 %multiply_reduce_fusion = (f32[512]{0:T(512)S(1)}, f32[512,512]{0,1:T(8,128)}) fusion(bf16[512,512]{0,1:T(8,128)(2,1)} %all_gather.11, bf16[512,512]{0,1:T(8,128)(2,1)S(1)} %all_gather.10, bf16[512,512]{1,0:T(8,128)(2,1)S(1)} %copy-done, f32[512,512]{1,0:T(8,128)} %convolution_bitcast_fusion.1), kind=kOutput, calls=%fused_computation.28 | convolution fusion | flops 538967552 | bytes 3672064 | tf_op jit(solution)/shard_map/dot_general | solution.py:123
  243.4 2.5 copy.25
  246.0 1.7 maximum_maximum_fusion
  247.8 1.8 fusion.30
  249.6 0.0 copy-start.15
  249.6 1.9 fusion.5
  251.6 3.1 %fusion.9 = bf16[512,512]{1,0:T(8,128)(2,1)} fusion(bf16[2,1536,512]{2,1,0:T(8,128)(2,1)S(1)} %maximum_maximum_fusion, f32[512,1536]{0,1:T(8,128)S(1)} %get-tuple-element.11, f32[512]{0:T(512)S(1)} %fusion.5, f32[512]{0:T(512)S(1)} %get-tuple-element.10, f32[512,512]{1,0:T(8,128)S(1)} %copy-done.4, f32[512]{0:T(512)S(1)} %copy-done.15, ...), kind=kOutput, calls=%fused_computation.19 | convolution fusion | flops 815005696 | bytes 6322176 | tf_op jit(solution)/shard_map/dot_general | solution.py:31
  (37 shorter events, 0.1 us)
Async XLA Ops:
  7.2 231.5 %copy-start = (bf16[512,512]{1,0:T(8,128)(2,1)S(1)}, bf16[512,512]{1,0:T(8,128)(2,1)}, u32[]{:S(2)}) copy-start(bf16[512,512]{1,0:T(8,128)(2,1)} %param.12) | copy-start | bytes 1572868
  7.2 3.9 %copy-start.1 = (bf16[512,512]{1,0:T(8,128)(2,1)S(1)}, bf16[512,512]{1,0:T(8,128)(2,1)}, u32[]{:S(2)}) copy-start(bf16[512,512]{1,0:T(8,128)(2,1)} %param.13) | copy-start | bytes 1572868
  7.2 69.0 %reduce-scatter.6.cloned.1.call-start = ((), (), s32[]{:S(2)}) async-start(), calls=%async_computation.4 | async-start | bytes 557056 | tf_op jit(solution)/shard_map/reduce_scatter | solution.py:96
  9.0 2.1 copy-start.3
  11.1 1.4 copy-start.6
  12.4 125.7 %reduce-scatter.4.cloned.1.call-start = ((), (), s32[]{:S(2)}) async-start(), calls=%async_computation.3 | async-start | bytes 557056 | tf_op jit(solution)/shard_map/reduce_scatter | solution.py:93
  12.9 1.0 copy-start.5
  13.9 2.9 %copy-start.2 = (bf16[512,512]{1,0:T(8,128)(2,1)S(1)}, bf16[512,512]{1,0:T(8,128)(2,1)}, u32[]{:S(2)}) copy-start(bf16[512,512]{1,0:T(8,128)(2,1)} %param.14) | copy-start | bytes 1572868
  13.9 11.9 %copy-start.14 = (f32[512]{0:T(512)S(1)}, f32[512]{0:T(512)}, u32[]{:S(2)}) copy-start(f32[512]{0:T(512)} %param.15) | copy-start | bytes 6148
  16.8 183.3 %reduce-scatter.8.cloned.1.call-start = ((), (), s32[]{:S(2)}) async-start(), calls=%async_computation.5 | async-start | bytes 557056 | tf_op jit(solution)/shard_map/reduce_scatter | solution.py:99
  17.0 14.6 %copy-start.16 = (s32[4]{0:T(128)S(1)}, s32[4]{0:T(128)}, u32[]{:S(2)}) copy-start(s32[4]{0:T(128)} %param.16) | copy-start | bytes 52
  17.0 229.0 %collective-permute-start.1 = (bf16[2,512,512]{2,1,0:T(8,128)(2,1)S(1)}, bf16[2,512,512]{2,1,0:T(8,128)(2,1)}, u32[]{:S(2)}, u32[]{:S(2)}) collective-permute-start(bf16[2,512,512]{2,1,0:T(8,128)(2,1)S(1)} %pad_maximum_fusion), channel_id=1, source_target_pairs={{0,32},{32,64},{64,96},{96,128},{128,160},{160,192},{192,224},{224... | collective-permute-start | bytes 3145736 | tf_op jit(solution)/shard_map/ppermute | solution.py:14
  21.6 224.5 %collective-permute-start = (bf16[2,512,512]{2,1,0:T(8,128)(2,1)S(1)}, bf16[2,512,512]{2,1,0:T(8,128)(2,1)}, u32[]{:S(2)}, u32[]{:S(2)}) collective-permute-start(bf16[2,512,512]{2,1,0:T(8,128)(2,1)S(1)} %pad_maximum_fusion), channel_id=1, source_target_pairs={{0,64},{32,96},{64,128},{96,160},{128,192},{160,224},{192,256},{22... | collective-permute-start | bytes 3145736 | tf_op jit(solution)/shard_map/ppermute | solution.py:14
  28.9 2.8 %copy-start.10 = (s32[512]{0:T(512)}, s32[512]{0:T(512)S(1)}, u32[]{:S(2)}) copy-start(s32[512]{0:T(512)S(1)} %iota_add_fusion.1) | copy-start | bytes 6148
  77.2 166.2 %copy-start.7 = (f32[512,32]{0,1:T(8,128)}, f32[512,32]{0,1:T(8,128)S(1)}, u32[]{:S(2)}) copy-start(f32[512,32]{0,1:T(8,128)S(1)} %get-tuple-element.7) | copy-start | bytes 196612
  139.1 104.3 %copy-start.8 = (f32[512,32]{0,1:T(8,128)}, f32[512,32]{0,1:T(8,128)S(1)}, u32[]{:S(2)}) copy-start(f32[512,32]{0,1:T(8,128)S(1)} %get-tuple-element.5) | copy-start | bytes 196612
  201.1 42.3 %copy-start.9 = (f32[512,32]{0,1:T(8,128)}, f32[512,32]{0,1:T(8,128)S(1)}, u32[]{:S(2)}) copy-start(f32[512,32]{0,1:T(8,128)S(1)} %get-tuple-element.9) | copy-start | bytes 196612
  246.0 1.8 copy-start.11
  246.0 1.8 copy-start.12
  246.0 1.8 copy-start.13
  249.6 1.9 copy-start.4
  249.6 1.9 copy-start.15
Sparse Core Ops, SparseCore 0:
  12.6 63.6 reduce-scatter.5
  79.0 59.0 reduce-scatter.3
  141.5 58.6 reduce-scatter.7
where the time goes:
time: 262 us; the launch traced here: 261 us
  waiting for transfers between devices  147 us (56%)
  blocking collectives  54.5 us (21%)
  matrix products  21.2 us (8%)
  between operations  14.1 us (5%)
  other arithmetic  9.19 us (4%)
  starting transfers between devices  8.92 us (3%)
  local copies, waits for them, and re-layouts  6.51 us (2%)
    reduce_scatter x1, waiting for transfers between devices, local(): lax.psum_scatter(part_gate.astype(jnp.bfloat16), 'seq', scatter_dimension...  60.9 us
    reduce_scatter x1, waiting for transfers between devices, local(): lax.psum_scatter(part_down.astype(jnp.bfloat16), 'seq', scatter_dimension...  43.1 us
    reduce_scatter x1, waiting for transfers between devices, local(): lax.psum_scatter(part_up.astype(jnp.bfloat16), 'seq', scatter_dimension=1...  42.8 us
    all_gather x1, blocking collectives, local(): lax.all_gather(shard_down, 'seq', axis=1, tiled=True)  19.3 us
    all_gather x1, blocking collectives, local(): lax.all_gather(shard_up, 'seq', axis=1, tiled=True)  17.9 us
    all_gather x1, blocking collectives, local(): lax.all_gather(shard_gate, 'seq', axis=1, tiled=True)  17.4 us
    ppermute x2, starting transfers between devices, shifted(): return lax.ppermute(block, axis, route)  8.8 us
  transfers between devices with their start and end apart: 5, of which 3 were waited for; matrix products, arithmetic and copies ran while one was open for 8% of the time, Pallas kernels for 0%

commit v1 on v0

--- a/solution.py
+++ b/solution.py
@@ -6,6 +6,24 @@
 WIN = 1024
 momentum_decay = 0.9
 step_size = 0.5
+
+
+def collect(shard, axis, dim):
+    ways, here, lap = (lax.axis_size(axis), lax.axis_index(axis), shard.shape[dim])
+    dims = [n * ways if d == dim else n for d, n in enumerate(shard.shape)]
+    full = lax.dynamic_update_slice_in_dim(
+        jnp.zeros(dims, shard.dtype), shard, here * lap, axis=dim
+    )
+    going_up = going_down = shard
+    for far in range(1, ways // 2 + 1):
+        going_up = lax.ppermute(going_up, axis, [(d, (d + 1) % ways) for d in range(ways)])
+        full = lax.dynamic_update_slice_in_dim(full, going_up, (here - far) % ways * lap, axis=dim)
+        if 2 * far < ways:
+            going_down = lax.ppermute(going_down, axis, [(d, (d - 1) % ways) for d in range(ways)])
+            full = lax.dynamic_update_slice_in_dim(
+                full, going_down, (here + far) % ways * lap, axis=dim
+            )
+    return full
 
 
 def shifted(block, axis, distance):
@@ -115,7 +133,7 @@
     gate_new, up_new, down_new = (
         lax.all_gather(shard_gate, "seq", axis=1, tiled=True),
         lax.all_gather(shard_up, "seq", axis=1, tiled=True),
-        lax.all_gather(shard_down, "seq", axis=1, tiled=True),
+        collect(shard_down, "seq", 1),
     )
     qa = jnp.dot(queries, gate_new, preferred_element_type=jnp.float32)
     qb = jnp.dot(queries, up_new, preferred_element_type=jnp.float32)

time: 262 us -> 282 us (1.076)
  starting transfers between devices: 8.92 us -> 30.3 us
  blocking collectives: 54.5 us -> 36.6 us
  waiting for transfers between devices: 147 us -> 162 us
    ppermute x0 -> x15, starting transfers between devices: none -> 21.3 us  [the longest x7 17.3 us: collect(): lax.ppermute(going_down, axis, [(d, (d - 1) % ways) for d in range(ways)])]
    all_gather x1 -> x0, blocking collectives: 19.3 us -> none  [local(): lax.all_gather(shard_down, 'seq', axis=1, tiled=True)]
    ppermute x0 -> x15, waiting for transfers between devices: none -> 9.04 us  [the longest x8 8.46 us: collect(): lax.ppermute(going_up, axis, [(d, (d + 1) % ways) for d in range(ways)])]
    reduce_scatter x1, waiting for transfers between devices: 42.8 us -> 51.6 us  [local(): lax.psum_scatter(part_up.astype(jnp.bfloat16), 'seq', scatter_dimension=1...]
    reduce_scatter x1, waiting for transfers between devices: 60.9 us -> 55.8 us  [local(): lax.psum_scatter(part_gate.astype(jnp.bfloat16), 'seq', scatter_dimension...]
  transfers between devices with their start and end apart: 5 -> 20, of which waited for: 3 -> 14; matrix products, arithmetic and copies ran while one was open for 8% -> 8% of each run, Pallas kernels for 0% -> 0%
where the time goes in v1:
time: 282 us; the launch traced here: 279 us
  waiting for transfers between devices  162 us (57%)
  blocking collectives  36.6 us (13%)
  starting transfers between devices  30.3 us (11%)
  matrix products  21.3 us (8%)
  between operations  14.5 us (5%)
  other arithmetic  8.9 us (3%)
  local copies, waits for them, and re-layouts  5.81 us (2%)
    reduce_scatter x1, waiting for transfers between devices, local(): lax.psum_scatter(part_gate.astype(jnp.bfloat16), 'seq', scatter_dimension...  55.8 us
    reduce_scatter x1, waiting for transfers between devices, local(): lax.psum_scatter(part_up.astype(jnp.bfloat16), 'seq', scatter_dimension=1...  51.6 us
    reduce_scatter x1, waiting for transfers between devices, local(): lax.psum_scatter(part_down.astype(jnp.bfloat16), 'seq', scatter_dimension...  45.3 us
    all_gather x1, blocking collectives, local(): lax.all_gather(shard_up, 'seq', axis=1, tiled=True)  18.7 us
    all_gather x1, blocking collectives, local(): lax.all_gather(shard_gate, 'seq', axis=1, tiled=True)  17.9 us
    ppermute x7, starting transfers between devices, collect(): lax.ppermute(going_down, axis, [(d, (d - 1) % ways) for d in range(ways)])  17.3 us
    ppermute x2, starting transfers between devices, shifted(): return lax.ppermute(block, axis, route)  8.89 us
    ppermute x8, waiting for transfers between devices, collect(): lax.ppermute(going_up, axis, [(d, (d + 1) % ways) for d in range(ways)])  8.46 us
  transfers between devices with their start and end apart: 20, of which 14 were waited for; matrix products, arithmetic and copies ran while one was open for 8% of the time, Pallas kernels for 0%

profile of v1, /device:TPU:1, one launch (start us, length us, event | category | flops | bytes accessed | tf_op | source)
XLA Modules:
  0.0 279.1 jit_solution(14308296063035355260)
XLA Ops:
  7.2 1.7 fusion.29
  9.0 2.0 fusion.30
  11.0 1.0 copy-done.6
  12.0 1.5 convolution_convert_fusion
  13.6 0.5 fusion.21
  14.1 2.5 fusion.11
  16.7 1.1 pad_maximum_fusion
  17.8 4.7 %collective-permute-start.1 = (bf16[2,512,512]{2,1,0:T(8,128)(2,1)}, bf16[2,512,512]{2,1,0:T(8,128)(2,1)}, u32[]{:S(2)}, u32[]{:S(2)}) collective-permute-start(bf16[2,512,512]{2,1,0:T(8,128)(2,1)} %pad_maximum_fusion), channel_id=1, source_target_pairs={{0,32},{32,64},{64,96},{96,128},{128,160},{160,192},{192,224},{224... | collective-permute-start | bytes 3145736 | tf_op jit(solution)/shard_map/ppermute | solution.py:32
  22.5 4.2 %collective-permute-start = (bf16[2,512,512]{2,1,0:T(8,128)(2,1)}, bf16[2,512,512]{2,1,0:T(8,128)(2,1)}, u32[]{:S(2)}, u32[]{:S(2)}) collective-permute-start(bf16[2,512,512]{2,1,0:T(8,128)(2,1)} %pad_maximum_fusion), channel_id=1, source_target_pairs={{0,64},{32,96},{64,128},{96,160},{128,192},{160,224},{192,256},{22... | collective-permute-start | bytes 3145736 | tf_op jit(solution)/shard_map/ppermute | solution.py:32
  26.7 3.1 %fusion.10 = bf16[512,512]{0,1:T(8,128)(2,1)} fusion(bf16[512,512]{1,0:T(8,128)(2,1)S(1)} %copy-done.1, f32[512,512]{1,0:T(8,128)} %copy-done.6, f32[512,512]{1,0:T(8,128)S(1)} %fusion.21, f32[512,512]{1,0:T(8,128)} %copy-done.5), kind=kOutput, calls=%fused_computation.23 | convolution fusion | flops 271319040 | bytes 4194304 | tf_op jit(solution)/shard_map/dot_general | solution.py:104
  29.9 1.1 constant_dynamic-slice_fusion.1
  31.3 0.2 reduce-window.8
  32.0 45.3 %reduce-scatter.8.cloned.1.call-done = bf16[512,32]{0,1:T(8,128)(2,1)} async-done(((bf16[512,512]{0,1:T(8,128)(2,1)}), bf16[512,32]{0,1:T(8,128)(2,1)}) %reduce-scatter.8.cloned.1.call-update) | async-done | bytes 32784 | tf_op jit(solution)/shard_map/reduce_scatter | solution.py:117
  77.4 0.9 multiply_reduce_fusion.1
  78.4 0.4 collective-permute-start.2
  78.8 1.9 collective-permute-start.3
  80.6 1.7 maximum_maximum_fusion
  82.4 1.8 fusion.28
  84.2 1.6 copy-done.4
  85.8 1.9 fusion.5
  87.7 51.6 %reduce-scatter.6.cloned.1.call-done = bf16[512,32]{0,1:T(8,128)(2,1)} async-done(((bf16[512,512]{0,1:T(8,128)(2,1)}), bf16[512,32]{0,1:T(8,128)(2,1)}) %reduce-scatter.6.cloned.1.call-update) | async-done | bytes 32784 | tf_op jit(solution)/shard_map/reduce_scatter | solution.py:114
  139.3 0.9 multiply_reduce_fusion.2
  140.2 4.7 %fusion.6 = f32[512,512]{1,0:T(8,128)S(1)} fusion(bf16[2,1536,512]{2,1,0:T(8,128)(2,1)} %copy-done.3, f32[512,1536]{0,1:T(8,128)} %copy-done.4, f32[512]{0:T(512)S(1)} %fusion.5, f32[512]{0:T(512)S(1)} %get-tuple-element.12, s32[1536]{0:T(1024)S(1)} %iota_add_fusion, s32[512]{0:T(512)S(1)} %iota_add_fusion.1, s32[512]{0:T(512)S(1)} %convert_reduce_fusion.1, ...), kind=kOutput, calls=%fused_computation.13 | convolution fusion | flops 813957120 | bytes 5789184 | tf_op jit(solution)/shard_map/dot_general | solution.py:49
  144.9 55.8 %reduce-scatter.4.cloned.1.call-done = bf16[512,32]{0,1:T(8,128)(2,1)} async-done(((bf16[512,512]{0,1:T(8,128)(2,1)}), bf16[512,32]{0,1:T(8,128)(2,1)}) %reduce-scatter.4.cloned.1.call-update) | async-done | bytes 32784 | tf_op jit(solution)/shard_map/reduce_scatter | solution.py:111
  200.7 0.9 multiply_reduce_fusion.3
  201.7 17.9 %all_gather.6 = bf16[512,512]{0,1:T(8,128)(2,1)S(1)} all-gather(bf16[512,32]{0,1:T(8,128)(2,1)S(1)} %subtract_convert_fusion.2), channel_id=1, replica_groups=mesh['seq'=16,'doc'=32] {'seq'}, dimensions={1}, use_global_device_ids=true | all-gather | bytes 557056 | tf_op jit(solution)/shard_map/all_gather | solution.py:134
  219.6 0.5 convolution_bitcast_fusion.1
  220.2 18.7 %all_gather.7 = bf16[512,512]{0,1:T(8,128)(2,1)} all-gather(bf16[512,32]{0,1:T(8,128)(2,1)S(1)} %subtract_convert_fusion.1), channel_id=1, replica_groups=mesh['seq'=16,'doc'=32] {'seq'}, dimensions={1}, use_global_device_ids=true | all-gather | bytes 557056 | tf_op jit(solution)/shard_map/all_gather | solution.py:135
  238.9 0.5 collective-permute-start.5
  239.4 0.7 collective-permute-done.4
  240.1 2.2 collective-permute-start.6
  242.2 1.4 collective-permute-start.7
  243.6 0.7 collective-permute-done.6
  244.3 1.3 collective-permute-start.8
  245.6 2.6 collective-permute-start.9
  248.2 0.7 collective-permute-done.8
  249.0 3.7 %collective-permute-start.11 = (bf16[512,32]{0,1:T(8,128)(2,1)S(1)}, bf16[512,32]{0,1:T(8,128)(2,1)S(1)}, u32[]{:S(2)}, u32[]{:S(2)}) collective-permute-start(bf16[512,32]{0,1:T(8,128)(2,1)S(1)} %collective-permute-done.9), channel_id=1, source_target_pairs={{0,480},{32,0},{64,32},{96,64},{128,96},{160,128},{192,160},{224,1... | collective-permute-start | bytes 98312 | tf_op jit(solution)/shard_map/ppermute | solution.py:22
  252.7 0.7 collective-permute-done.10
  253.4 0.2 collective-permute-done.11
  253.6 3.7 %collective-permute-start.13 = (bf16[512,32]{0,1:T(8,128)(2,1)S(1)}, bf16[512,32]{0,1:T(8,128)(2,1)S(1)}, u32[]{:S(2)}, u32[]{:S(2)}) collective-permute-start(bf16[512,32]{0,1:T(8,128)(2,1)S(1)} %collective-permute-done.11), channel_id=1, source_target_pairs={{0,480},{32,0},{64,32},{96,64},{128,96},{160,128},{192,160},{224,1... | collective-permute-start | bytes 98312 | tf_op jit(solution)/shard_map/ppermute | solution.py:22
  257.3 0.7 collective-permute-done.12
  257.9 0.2 collective-permute-done.13
  258.1 3.7 %collective-permute-start.15 = (bf16[512,32]{0,1:T(8,128)(2,1)S(1)}, bf16[512,32]{0,1:T(8,128)(2,1)S(1)}, u32[]{:S(2)}, u32[]{:S(2)}) collective-permute-start(bf16[512,32]{0,1:T(8,128)(2,1)S(1)} %collective-permute-done.13), channel_id=1, source_target_pairs={{0,480},{32,0},{64,32},{96,64},{128,96},{160,128},{192,160},{224,1... | collective-permute-start | bytes 98312 | tf_op jit(solution)/shard_map/ppermute | solution.py:22
  261.8 0.7 collective-permute-done.14
  262.7 4.4 %collective-permute-done.16 = bf16[512,32]{0,1:T(8,128)(2,1)S(1)} collective-permute-done((bf16[512,32]{0,1:T(8,128)(2,1)S(1)}, bf16[512,32]{0,1:T(8,128)(2,1)S(1)}, u32[]{:S(2)}, u32[]{:S(2)}) %collective-permute-start.16) | collective-permute-done | bytes 32800 | tf_op jit(solution)/shard_map/ppermute | solution.py:19
  267.1 3.0 %multiply_reduce_fusion = (f32[512]{0:T(512)S(1)}, f32[512,512]{0,1:T(8,128)}) fusion(bf16[512,512]{0,1:T(8,128)(2,1)S(1)} %constant_dynamic-update-slice_fusion, bf16[512,512]{0,1:T(8,128)(2,1)} %all_gather.7, bf16[512,512]{1,0:T(8,128)(2,1)S(1)} %copy-done, f32[512,512]{1,0:T(8,128)S(1)} %convolution_bitcast_fusion.1), kind=kOutput, calls=%fused_computation.27 | convolution fusion | flops 538967552 | bytes 3672064 | tf_op jit(solution)/shard_map/dot_general | solution.py:141
  270.0 1.6 copy.25
  271.6 1.0 add_convert_fusion
  (83 shorter events, 1.5 us)
Async XLA Ops:
  7.2 75.2 %copy-start = (bf16[512,512]{1,0:T(8,128)(2,1)S(1)}, bf16[512,512]{1,0:T(8,128)(2,1)}, u32[]{:S(2)}) copy-start(bf16[512,512]{1,0:T(8,128)(2,1)} %param.12) | copy-start | bytes 1572868
  7.2 4.8 %copy-start.2 = (bf16[512,512]{1,0:T(8,128)(2,1)S(1)}, bf16[512,512]{1,0:T(8,128)(2,1)}, u32[]{:S(2)}) copy-start(bf16[512,512]{1,0:T(8,128)(2,1)} %param.14) | copy-start | bytes 1572868
  7.2 4.8 %copy-start.14 = (f32[512]{0:T(512)S(1)}, f32[512]{0:T(512)}, u32[]{:S(2)}) copy-start(f32[512]{0:T(512)} %param.15) | copy-start | bytes 6148
  7.2 70.2 %reduce-scatter.8.cloned.1.call-start = ((), (), s32[]{:S(2)}) async-start(), calls=%async_computation.5 | async-start | bytes 557056 | tf_op jit(solution)/shard_map/reduce_scatter | solution.py:117
  9.0 2.0 copy-start.5
  11.0 1.0 copy-start.6
  12.0 1.6 copy-start.7
  12.0 2.1 copy-start.1
  13.5 125.7 %reduce-scatter.6.cloned.1.call-start = ((), (), s32[]{:S(2)}) async-start(), calls=%async_computation.4 | async-start | bytes 557056 | tf_op jit(solution)/shard_map/reduce_scatter | solution.py:114
  16.7 184.0 %reduce-scatter.4.cloned.1.call-start = ((), (), s32[]{:S(2)}) async-start(), calls=%async_computation.3 | async-start | bytes 557056 | tf_op jit(solution)/shard_map/reduce_scatter | solution.py:111
  17.8 13.5 %copy-start.16 = (s32[4]{0:T(128)S(1)}, s32[4]{0:T(128)}, u32[]{:S(2)}) copy-start(s32[4]{0:T(128)} %param.16) | copy-start | bytes 52
  17.8 59.6 %copy-start.11 = (f32[512,32]{0,1:T(8,128)S(1)}, f32[512,32]{0,1:T(8,128)}, u32[]{:S(2)}) copy-start(f32[512,32]{0,1:T(8,128)} %param.23) | copy-start | bytes 196612
  17.8 62.8 %collective-permute-start.1 = (bf16[2,512,512]{2,1,0:T(8,128)(2,1)}, bf16[2,512,512]{2,1,0:T(8,128)(2,1)}, u32[]{:S(2)}, u32[]{:S(2)}) collective-permute-start(bf16[2,512,512]{2,1,0:T(8,128)(2,1)} %pad_maximum_fusion), channel_id=1, source_target_pairs={{0,32},{32,64},{64,96},{96,128},{128,160},{160,192},{192,224},{224... | collective-permute-start | bytes 3145736 | tf_op jit(solution)/shard_map/ppermute | solution.py:32
  22.5 58.1 %collective-permute-start = (bf16[2,512,512]{2,1,0:T(8,128)(2,1)}, bf16[2,512,512]{2,1,0:T(8,128)(2,1)}, u32[]{:S(2)}, u32[]{:S(2)}) collective-permute-start(bf16[2,512,512]{2,1,0:T(8,128)(2,1)} %pad_maximum_fusion), channel_id=1, source_target_pairs={{0,64},{32,96},{64,128},{96,160},{128,192},{160,224},{192,256},{22... | collective-permute-start | bytes 3145736 | tf_op jit(solution)/shard_map/ppermute | solution.py:32
  78.2 4.1 %copy-start.8 = (f32[512,32]{0,1:T(8,128)}, f32[512,32]{0,1:T(8,128)S(1)}, u32[]{:S(2)}) copy-start(f32[512,32]{0,1:T(8,128)S(1)} %get-tuple-element.11) | copy-start | bytes 196612
  78.4 160.5 %collective-permute-start.2 = (bf16[512,32]{0,1:T(8,128)(2,1)S(1)}, bf16[512,32]{0,1:T(8,128)(2,1)S(1)}, u32[]{:S(2)}, u32[]{:S(2)}) collective-permute-start(bf16[512,32]{0,1:T(8,128)(2,1)S(1)} %get-tuple-element.9), channel_id=1, source_target_pairs={{0,32},{32,64},{64,96},{96,128},{128,160},{160,192},{192,224},{224... | collective-permute-start | bytes 98312 | tf_op jit(solution)/shard_map/ppermute | solution.py:19
  78.8 160.2 %collective-permute-start.3 = (bf16[512,32]{0,1:T(8,128)(2,1)S(1)}, bf16[512,32]{0,1:T(8,128)(2,1)S(1)}, u32[]{:S(2)}, u32[]{:S(2)}) collective-permute-start(bf16[512,32]{0,1:T(8,128)(2,1)S(1)} %get-tuple-element.9), channel_id=1, source_target_pairs={{0,480},{32,0},{64,32},{96,64},{128,96},{160,128},{192,160},{224,1... | collective-permute-start | bytes 98312 | tf_op jit(solution)/shard_map/ppermute | solution.py:22
  82.4 1.8 copy-start.3
  84.2 1.7 copy-start.4
  84.2 55.1 %copy-start.12 = (f32[512,32]{0,1:T(8,128)S(1)}, f32[512,32]{0,1:T(8,128)}, u32[]{:S(2)}) copy-start(f32[512,32]{0,1:T(8,128)} %param.22) | copy-start | bytes 196612
  140.2 79.9 %copy-start.9 = (f32[512,32]{0,1:T(8,128)}, f32[512,32]{0,1:T(8,128)S(1)}, u32[]{:S(2)}) copy-start(f32[512,32]{0,1:T(8,128)S(1)} %get-tuple-element.7) | copy-start | bytes 196612
  140.2 60.5 %copy-start.13 = (f32[512,32]{0,1:T(8,128)S(1)}, f32[512,32]{0,1:T(8,128)}, u32[]{:S(2)}) copy-start(f32[512,32]{0,1:T(8,128)} %param.21) | copy-start | bytes 196612
  201.6 68.4 %copy-start.10 = (f32[512,32]{0,1:T(8,128)}, f32[512,32]{0,1:T(8,128)S(1)}, u32[]{:S(2)}) copy-start(f32[512,32]{0,1:T(8,128)S(1)} %get-tuple-element.5) | copy-start | bytes 196612
  238.9 1.2 collective-permute-start.4
  238.9 3.3 %collective-permute-start.5 = (bf16[512,32]{0,1:T(8,128)(2,1)S(1)}, bf16[512,32]{0,1:T(8,128)(2,1)S(1)}, u32[]{:S(2)}, u32[]{:S(2)}) collective-permute-start(bf16[512,32]{0,1:T(8,128)(2,1)S(1)} %collective-permute-done.3), channel_id=1, source_target_pairs={{0,480},{32,0},{64,32},{96,64},{128,96},{160,128},{192,160},{224,1... | collective-permute-start | bytes 98312 | tf_op jit(solution)/shard_map/ppermute | solution.py:22
  240.1 4.2 %collective-permute-start.6 = (bf16[512,32]{0,1:T(8,128)(2,1)S(1)}, bf16[512,32]{0,1:T(8,128)(2,1)S(1)}, u32[]{:S(2)}, u32[]{:S(2)}) collective-permute-start(bf16[512,32]{0,1:T(8,128)(2,1)S(1)} %collective-permute-done.4), channel_id=1, source_target_pairs={{0,32},{32,64},{64,96},{96,128},{128,160},{160,192},{192,224},{224... | collective-permute-start | bytes 98312 | tf_op jit(solution)/shard_map/ppermute | solution.py:19
  242.2 3.3 %collective-permute-start.7 = (bf16[512,32]{0,1:T(8,128)(2,1)S(1)}, bf16[512,32]{0,1:T(8,128)(2,1)S(1)}, u32[]{:S(2)}, u32[]{:S(2)}) collective-permute-start(bf16[512,32]{0,1:T(8,128)(2,1)S(1)} %collective-permute-done.5), channel_id=1, source_target_pairs={{0,480},{32,0},{64,32},{96,64},{128,96},{160,128},{192,160},{224,1... | collective-permute-start | bytes 98312 | tf_op jit(solution)/shard_map/ppermute | solution.py:22
  244.3 4.6 %collective-permute-start.8 = (bf16[512,32]{0,1:T(8,128)(2,1)S(1)}, bf16[512,32]{0,1:T(8,128)(2,1)S(1)}, u32[]{:S(2)}, u32[]{:S(2)}) collective-permute-start(bf16[512,32]{0,1:T(8,128)(2,1)S(1)} %collective-permute-done.6), channel_id=1, source_target_pairs={{0,32},{32,64},{64,96},{96,128},{128,160},{160,192},{192,224},{224... | collective-permute-start | bytes 98312 | tf_op jit(solution)/shard_map/ppermute | solution.py:19
  245.6 3.4 %collective-permute-start.9 = (bf16[512,32]{0,1:T(8,128)(2,1)S(1)}, bf16[512,32]{0,1:T(8,128)(2,1)S(1)}, u32[]{:S(2)}, u32[]{:S(2)}) collective-permute-start(bf16[512,32]{0,1:T(8,128)(2,1)S(1)} %collective-permute-done.7), channel_id=1, source_target_pairs={{0,480},{32,0},{64,32},{96,64},{128,96},{160,128},{192,160},{224,1... | collective-permute-start | bytes 98312 | tf_op jit(solution)/shard_map/ppermute | solution.py:22
  248.8 4.6 %collective-permute-start.10 = (bf16[512,32]{0,1:T(8,128)(2,1)S(1)}, bf16[512,32]{0,1:T(8,128)(2,1)S(1)}, u32[]{:S(2)}, u32[]{:S(2)}) collective-permute-start(bf16[512,32]{0,1:T(8,128)(2,1)S(1)} %collective-permute-done.8), channel_id=1, source_target_pairs={{0,32},{32,64},{64,96},{96,128},{128,160},{160,192},{192,224},{224... | collective-permute-start | bytes 98312 | tf_op jit(solution)/shard_map/ppermute | solution.py:19
  249.0 4.6 %collective-permute-start.11 = (bf16[512,32]{0,1:T(8,128)(2,1)S(1)}, bf16[512,32]{0,1:T(8,128)(2,1)S(1)}, u32[]{:S(2)}, u32[]{:S(2)}) collective-permute-start(bf16[512,32]{0,1:T(8,128)(2,1)S(1)} %collective-permute-done.9), channel_id=1, source_target_pairs={{0,480},{32,0},{64,32},{96,64},{128,96},{160,128},{192,160},{224,1... | collective-permute-start | bytes 98312 | tf_op jit(solution)/shard_map/ppermute | solution.py:22
  253.4 4.6 %collective-permute-start.12 = (bf16[512,32]{0,1:T(8,128)(2,1)S(1)}, bf16[512,32]{0,1:T(8,128)(2,1)S(1)}, u32[]{:S(2)}, u32[]{:S(2)}) collective-permute-start(bf16[512,32]{0,1:T(8,128)(2,1)S(1)} %collective-permute-done.10), channel_id=1, source_target_pairs={{0,32},{32,64},{64,96},{96,128},{128,160},{160,192},{192,224},{224... | collective-permute-start | bytes 98312 | tf_op jit(solution)/shard_map/ppermute | solution.py:19
  253.6 4.6 %collective-permute-start.13 = (bf16[512,32]{0,1:T(8,128)(2,1)S(1)}, bf16[512,32]{0,1:T(8,128)(2,1)S(1)}, u32[]{:S(2)}, u32[]{:S(2)}) collective-permute-start(bf16[512,32]{0,1:T(8,128)(2,1)S(1)} %collective-permute-done.11), channel_id=1, source_target_pairs={{0,480},{32,0},{64,32},{96,64},{128,96},{160,128},{192,160},{224,1... | collective-permute-start | bytes 98312 | tf_op jit(solution)/shard_map/ppermute | solution.py:22
  257.9 4.6 %collective-permute-start.14 = (bf16[512,32]{0,1:T(8,128)(2,1)S(1)}, bf16[512,32]{0,1:T(8,128)(2,1)S(1)}, u32[]{:S(2)}, u32[]{:S(2)}) collective-permute-start(bf16[512,32]{0,1:T(8,128)(2,1)S(1)} %collective-permute-done.12), channel_id=1, source_target_pairs={{0,32},{32,64},{64,96},{96,128},{128,160},{160,192},{192,224},{224... | collective-permute-start | bytes 98312 | tf_op jit(solution)/shard_map/ppermute | solution.py:19
  258.1 4.6 %collective-permute-start.15 = (bf16[512,32]{0,1:T(8,128)(2,1)S(1)}, bf16[512,32]{0,1:T(8,128)(2,1)S(1)}, u32[]{:S(2)}, u32[]{:S(2)}) collective-permute-start(bf16[512,32]{0,1:T(8,128)(2,1)S(1)} %collective-permute-done.13), channel_id=1, source_target_pairs={{0,480},{32,0},{64,32},{96,64},{128,96},{160,128},{192,160},{224,1... | collective-permute-start | bytes 98312 | tf_op jit(solution)/shard_map/ppermute | solution.py:22
  262.5 4.6 %collective-permute-start.16 = (bf16[512,32]{0,1:T(8,128)(2,1)S(1)}, bf16[512,32]{0,1:T(8,128)(2,1)S(1)}, u32[]{:S(2)}, u32[]{:S(2)}) collective-permute-start(bf16[512,32]{0,1:T(8,128)(2,1)S(1)} %collective-permute-done.14), channel_id=1, source_target_pairs={{0,32},{32,64},{64,96},{96,128},{128,160},{160,192},{192,224},{224... | collective-permute-start | bytes 98312 | tf_op jit(solution)/shard_map/ppermute | solution.py:19
  267.0 4.6 %copy-start.15 = (f32[512]{0:T(512)S(1)}, f32[512]{0:T(512)}, u32[]{:S(2)}) copy-start(f32[512]{0:T(512)} %param.17) | copy-start | bytes 6148
Sparse Core Ops, SparseCore 0:
  13.7 63.6 reduce-scatter.7
  80.1 59.1 reduce-scatter.5
  142.1 58.5 reduce-scatter.3
